TPU v7x, 256 devices: a whole 4x4x8 slice. The times are simulated.
256 devices in a mesh: dp: 32 (over z, x_hi, core), tensor: 8 (over y, x_lo).
Axes of the slice: x: 4 (x_hi: 2, x_lo: 2; x = x_hi * 2 + x_lo), y: 4, z: 8, core: 2. Of those that a mesh axis runs over, the one named last changes fastest.
Arguments:
- context: bfloat16 [12288, 8192], P('dp', 'tensor'), may hold values from -6 to 6
- output_weight: bfloat16 [8192, 8192], P('tensor', 'dp'), may hold values from -0.0625 to 0.0625
- adapter_down_weight: bfloat16 [8192, 16], P('tensor'), may hold values from -0.0625 to 0.0625
- adapter_up_weight: bfloat16 [16, 8192], replicated, may hold values from -0.29882812 to 0.29882812
- residual: bfloat16 [12288, 8192], P('dp', 'tensor'), may hold values from -60 to 60
- frozen_residual_delta: bfloat16 [12288, 8192], P('dp', 'tensor'), may hold values from -6 to 6
- harmful_count: int32 [32], replicated, may hold values from 48 to 192
- retain_count: int32 [32], replicated, may hold values from 48 to 192
Outputs:
- adapted: bfloat16 [12288, 8192], P('dp', 'tensor')
- grad_a: float32 [8192, 16], P('tensor')
- grad_b: float32 [16, 8192], replicated
All inputs are finite; a program needn't handle non-finite values.
Results may differ from a plain program's by a relative error of at most 0.005.
Values may be sent and summed in bfloat16 or wider, within the bound.
A program may use at most 128 MiB of HBM per device.

v0:
```python
import jax
import jax.numpy as jnp
from jax import lax
from jax.sharding import PartitionSpec as P

ADAPTER_SCALE = 2.0
NORM_EPS = 1e-06
REROUTE_WEIGHT = 65536.0
RETAIN_WEIGHT = 1024.0


def row_gradient(
    hidden_states,
    target,
    sq_state,
    sq_target,
    cross_term,
    gap_sq,
    harmful,
    retained,
    harm_total,
    keep_total,
):
    norm_h = jnp.sqrt(sq_state + NORM_EPS)
    norm_g = jnp.sqrt(sq_target + NORM_EPS)
    cosine = cross_term / (norm_h * norm_g)
    distance = jnp.sqrt(gap_sq + NORM_EPS)
    weight_harm = REROUTE_WEIGHT / harm_total * harmful
    weight_keep = RETAIN_WEIGHT / keep_total * retained
    first = (weight_harm / (norm_h * norm_g))[:, None] * target
    second = (weight_harm * cosine / (norm_h * norm_h))[:, None] * hidden_states
    third = (weight_keep / distance)[:, None] * (hidden_states - target)
    return first - second + third


def token_masks(positions, harm_here, keep_here):
    harmful = (positions < harm_here).astype(jnp.float32)
    retained = ((positions >= harm_here) & (positions < harm_here + keep_here)).astype(jnp.float32)
    return (harmful, retained)


def head_terms(context, output_weight):
    return jnp.dot(
        context,
        lax.all_gather(output_weight, "dp", axis=1, tiled=True),
        preferred_element_type=jnp.float32,
    )


def local(
    context,
    output_weight,
    adapter_down_weight,
    adapter_up_weight,
    residual,
    frozen_residual_delta,
    harmful_count,
    retain_count,
):
    seq_len = context.shape[0]
    tensor_rank = lax.axis_index("tensor")
    data_rank = lax.axis_index("dp")
    harm_total = jnp.sum(harmful_count).astype(jnp.float32)
    keep_total = jnp.sum(retain_count).astype(jnp.float32)
    harm_here = harmful_count[data_rank]
    keep_here = retain_count[data_rank]
    up_weight_single = adapter_up_weight.astype(jnp.float32)
    reduced_state = lax.psum(
        jnp.dot(context, adapter_down_weight, preferred_element_type=jnp.float32), "tensor"
    )
    attn_cols = lax.psum_scatter(
        head_terms(context, output_weight).astype(jnp.bfloat16),
        "tensor",
        scatter_dimension=1,
        tiled=True,
    ).astype(jnp.float32)
    col_count = attn_cols.shape[1]
    up_weight_columns = lax.dynamic_slice_in_dim(
        up_weight_single, tensor_rank * col_count, col_count, 1
    )
    hidden_states = (
        residual.astype(jnp.float32)
        + attn_cols
        + ADAPTER_SCALE * jnp.dot(reduced_state, up_weight_columns, precision=lax.Precision.HIGHEST)
    )
    target = residual.astype(jnp.float32) + frozen_residual_delta.astype(jnp.float32)
    gap = hidden_states - target
    sq_state, sq_target, cross_term, gap_sq = lax.psum(
        (
            jnp.sum(hidden_states * hidden_states, axis=1),
            jnp.sum(target * target, axis=1),
            jnp.sum(hidden_states * target, axis=1),
            jnp.sum(gap * gap, axis=1),
        ),
        "tensor",
    )
    positions = jnp.arange(seq_len, dtype=jnp.int32)
    harmful, retained = token_masks(positions, harm_here, keep_here)
    output_gradient = row_gradient(
        hidden_states,
        target,
        sq_state,
        sq_target,
        cross_term,
        gap_sq,
        harmful,
        retained,
        harm_total,
        keep_total,
    )
    reduced_gradient = lax.psum(
        ADAPTER_SCALE
        * jnp.dot(output_gradient, up_weight_columns.T, precision=lax.Precision.HIGHEST),
        "tensor",
    )
    local_a = jnp.dot(
        context.T,
        reduced_gradient,
        precision=lax.Precision.HIGHEST,
        preferred_element_type=jnp.float32,
    )
    shard_up_weight = ADAPTER_SCALE * jnp.dot(
        reduced_state.T, output_gradient, precision=lax.Precision.HIGHEST
    )
    grad_a, grad_b_cols = lax.psum((local_a, shard_up_weight), "dp")
    grad_b = lax.all_gather(grad_b_cols, "tensor", axis=1, tiled=True)
    adapted = hidden_states.astype(jnp.bfloat16)
    return (adapted, grad_a, grad_b)


def solution(mesh):
    return jax.shard_map(
        local,
        mesh=mesh,
        in_specs=(
            P("dp", "tensor"),
            P("tensor", "dp"),
            P("tensor", None),
            P(),
            P("dp", "tensor"),
            P("dp", "tensor"),
            P(),
            P(),
        ),
        out_specs=(P("dp", "tensor"), P("tensor", None), P()),
        check_vma=False,
    )
```

profile of v0, /device:TPU:2, one launch (start us, length us, event | category | flops | bytes accessed | tf_op | source)
XLA Modules:
  0.0 659.6 jit_solution(2326122769122141415)
XLA Ops:
  7.2 0.0 copy-start
  7.2 0.0 all-gather.2.cloned.1.call-start
  7.2 0.7 all-gather.2.cloned.1.call-update
  7.9 0.0 reduce-scatter.2.cloned.1.call-start
  8.0 156.6 %all-gather.2.cloned.1.call-done = bf16[1024,8192]{1,0:T(8,128)(2,1)} async-done(((bf16[1024,256]{1,0:T(8,128)(2,1)}), bf16[1024,8192]{1,0:T(8,128)(2,1)}) %all-gather.2.cloned.1.call-update) | async-done | bytes 16777232 | tf_op jit(solution)/shard_map/all_gather | solution.py:45
  164.5 0.0 copy-done
  164.5 14.3 %convolution_convert_fusion = bf16[384,8192]{1,0:T(8,128)(2,1)} fusion(bf16[384,1024]{1,0:T(8,128)(2,1)S(1)} %copy-done, bf16[1024,8192]{1,0:T(8,128)(2,1)} %all-gather.2.cloned.1.call-done), kind=kOutput, calls=%fused_computation | convolution fusion | flops 6445596672 | bytes 23855104 | tf_op jit(solution)/shard_map/dot_general | solution.py:43
  178.9 0.0 copy-start.3
  178.9 0.0 copy-start.4
  178.9 0.0 copy-start.2
  178.9 0.0 copy-start.1
  178.9 0.0 reduce-scatter.2.cloned.1.call-update
  178.9 0.0 all-reduce.4.cloned.1.call-start
  179.0 0.6 copy-done.3
  179.5 0.6 reduce_sum.58
  180.2 0.6 dynamic_slice.11
  180.8 0.0 copy-done.4
  180.8 0.6 reduce_sum.54
  181.5 0.6 dynamic_slice.10
  184.7 0.0 copy-done.2
  184.7 0.3 fusion.8
  185.0 32.4 %psum.56 = f32[384,16]{0,1:T(8,128)S(1)} all-reduce(f32[384,16]{0,1:T(8,128)S(1)} %fusion.8), channel_id=1, replica_groups=mesh['dp'=32,'tensor'=8] {'tensor'}, use_global_device_ids=true, to_apply=%region_1.0 | all-reduce | flops 6144 | bytes 49152 | tf_op jit(solution)/shard_map/psum | solution.py:68
  217.4 92.1 %reduce-scatter.2.cloned.1.call-done = bf16[384,1024]{1,0:T(8,128)(2,1)} async-done(((bf16[384,8192]{1,0:T(8,128)(2,1)}), bf16[384,1024]{1,0:T(8,128)(2,1)}) %reduce-scatter.2.cloned.1.call-update) | async-done | bytes 786448 | tf_op jit(solution)/shard_map/reduce_scatter | solution.py:71
  309.5 0.0 copy-done.1
  309.5 3.1 multiply_reduce_fusion.1
  312.6 17.1 %all-reduce.1 = (f32[384]{0:T(512)S(1)}, f32[384]{0:T(512)S(1)}, f32[384]{0:T(512)S(1)}, f32[384]{0:T(512)S(1)}) all-reduce(f32[384]{0:T(512)S(1)} %get-tuple-element.4, f32[384]{0:T(512)S(1)} %get-tuple-element.3, f32[384]{0:T(512)S(1)} %get-tuple-element.6, f32[384]{0:T(512)S(1)} %get-tuple-element.5), channel_id=1, replica_groups=mesh['dp'=32,'tensor'=8] {'tensor'}, use_global_device_ids=true, to_apply=%region_11.0 | all-reduce | flops 1536 | bytes 12288 | tf_op jit(solution)/shard_map/psum | solution.py:88
  329.8 0.7 select_divide_fusion
  330.4 2.7 multiply_add_fusion
  333.1 1.5 convolution_multiply_fusion.1
  334.6 1.6 convolution_multiply_fusion
  336.2 33.9 %psum.61 = f32[384,16]{1,0:T(8,128)S(1)} all-reduce(f32[384,16]{1,0:T(8,128)S(1)} %convolution_multiply_fusion), channel_id=1, replica_groups=mesh['dp'=32,'tensor'=8] {'tensor'}, use_global_device_ids=true, to_apply=%region_12.0 | all-reduce | flops 6144 | bytes 49152 | tf_op jit(solution)/shard_map/psum | solution.py:111
  370.2 1.1 convolution_bitcast_fusion
  371.3 0.0 all-reduce.4.cloned.1.call-update
  371.3 249.6 %all-reduce.4.cloned.1.call-done = (f32[1024,16]{0,1:T(8,128)}, f32[16,1024]{1,0:T(8,128)}) async-done(((f32[1024,16]{0,1:T(8,128)}, f32[16,1024]{1,0:T(8,128)}), (f32[1024,16]{0,1:T(8,128)}, f32[16,1024]{1,0:T(8,128)})) %all-reduce.4.cloned.1.call-update) | async-done | bytes 131088 | tf_op jit(solution)/shard_map/psum | solution.py:125
  620.9 29.9 %all_gather.7 = f32[16,8192]{1,0:T(8,128)S(1)} all-gather(f32[16,1024]{1,0:T(8,128)} %get-tuple-element.8), channel_id=1, replica_groups=mesh['dp'=32,'tensor'=8] {'tensor'}, dimensions={1}, use_global_device_ids=true | all-gather | bytes 589824 | tf_op jit(solution)/shard_map/all_gather | solution.py:126
  650.8 1.5 copy.14
  652.3 0.8 copy.15
Async XLA Ops:
  7.2 157.4 %copy-start = (bf16[384,1024]{1,0:T(8,128)(2,1)S(1)}, bf16[384,1024]{1,0:T(8,128)(2,1)}, u32[]{:S(2)}) copy-start(bf16[384,1024]{1,0:T(8,128)(2,1)} %param.8) | copy-start | bytes 2359300
  7.2 157.4 %all-gather.2.cloned.1.call-start = ((), (), s32[]{:S(2)}) async-start(), calls=%async_computation.1 | async-start | bytes 17301504 | tf_op jit(solution)/shard_map/all_gather | solution.py:45
  7.9 301.6 %reduce-scatter.2.cloned.1.call-start = ((), (), s32[]{:S(2)}) async-start(), calls=%async_computation.2 | async-start | bytes 7077888 | tf_op jit(solution)/shard_map/reduce_scatter | solution.py:71
  178.9 0.7 copy-start.3
  178.9 1.9 copy-start.4
  178.9 5.8 copy-start.2
  178.9 130.6 %copy-start.1 = (bf16[384,1024]{1,0:T(8,128)(2,1)S(1)}, bf16[384,1024]{1,0:T(8,128)(2,1)}, u32[]{:S(2)}) copy-start(bf16[384,1024]{1,0:T(8,128)(2,1)} %param.13) | copy-start | bytes 2359300
  178.9 442.0 %all-reduce.4.cloned.1.call-start = ((), (), s32[]{:S(2)}) async-start(), calls=%async_computation.3 | async-start | bytes 262144 | tf_op jit(solution)/shard_map/psum | solution.py:125
Sparse Core Ops, SparseCore 0:
  10.5 153.9 all-gather.1
  179.0 130.3 reduce-scatter.1
  371.4 249.4 all-reduce.3
where the time goes:
time: 660 us
  waiting for transfers between devices  499 us (76%)
  blocking collectives  113 us (17%)
  matrix products  22 us (3%)
  between operations  16.5 us (2%)
    psum x1, waiting for transfers between devices, local(): grad_a, grad_b_cols = lax.psum((local_a, shard_up_weight), 'dp')  250 us
    all_gather x1, waiting for transfers between devices, head_terms(): lax.all_gather(output_weight, 'dp', axis=1, tiled=True)  157 us
    reduce_scatter x1, waiting for transfers between devices, local(): lax.psum_scatter(head_terms(context, output_weight).astype(jnp.bfloat16),...  92.1 us
    psum x1, blocking collectives, local(): lax.psum(ADAPTER_SCALE * jnp.dot(output_gradient, up_weight_columns.T, pr...  33.9 us
    psum x1, blocking collectives, local(): lax.psum(jnp.dot(context, adapter_down_weight, preferred_element_type=jnp...  32.4 us
    all_gather x1, blocking collectives, local(): grad_b = lax.all_gather(grad_b_cols, 'tensor', axis=1, tiled=True)  29.9 us
    psum x1, blocking collectives, local(): lax.psum((jnp.sum(hidden_states * hidden_states, axis=1), jnp.sum(target...  17.1 us
    dot_general x1, matrix products, head_terms(): jnp.dot(context, lax.all_gather(output_weight, 'dp', axis=1, tiled=True),...  14.3 us
  transfers between devices with their start and end apart: 3, of which 3 were waited for; matrix products, arithmetic and copies ran while one was open for 0% of the time, Pallas kernels for 0%

commit v1 on v0

--- a/solution.py
+++ b/solution.py
@@ -1,12 +1,27 @@
+import functools
 import jax
 import jax.numpy as jnp
 from jax import lax
 from jax.sharding import PartitionSpec as P
+from jax.lax import all_to_all, psum
 
 ADAPTER_SCALE = 2.0
 NORM_EPS = 1e-06
 REROUTE_WEIGHT = 65536.0
 RETAIN_WEIGHT = 1024.0
+
+
+def link_group(q_in, where_dim):
+    passed = jnp.concatenate(
+        all_to_all(
+            jnp.stack([q_in] * psum(1, axis_name="dp")), concat_axis=0, axis_name="dp", split_axis=0
+        ),
+        axis=where_dim,
+    )
+    return passed
+
+
+_draft_words = functools.partial(link_group, where_dim=1)
 
 
 def row_gradient(
@@ -40,11 +55,7 @@
 
 
 def head_terms(context, output_weight):
-    return jnp.dot(
-        context,
-        lax.all_gather(output_weight, "dp", axis=1, tiled=True),
-        preferred_element_type=jnp.float32,
-    )
+    return jnp.dot(context, _draft_words(output_weight), preferred_element_type=jnp.float32)
 
 
 def local(

time: 660 us -> 881 us (1.33)
  blocking collectives: 113 us -> 490 us
  waiting for transfers between devices: 499 us -> 342 us
    all_to_all x0 -> x1, blocking collectives: none -> 376 us  [link_group(): all_to_all(jnp.stack([q_in] * psum(1, axis_name='dp')), concat_axis=0, ax...]
    all_gather x1 -> x0, waiting for transfers between devices: 157 us -> none  [head_terms(): lax.all_gather(output_weight, 'dp', axis=1, tiled=True)]
  transfers between devices with their start and end apart: 3 -> 2, of which waited for: 3 -> 2; matrix products, arithmetic and copies ran while one was open for 0% -> 0% of each run, Pallas kernels for 0% -> 0%
where the time goes in v1:
time: 881 us
  blocking collectives  490 us (56%)
  waiting for transfers between devices  342 us (39%)
  matrix products  19.6 us (2%)
  between operations  16.8 us (2%)
    all_to_all x1, blocking collectives, link_group(): all_to_all(jnp.stack([q_in] * psum(1, axis_name='dp')), concat_axis=0, ax...  376 us
    psum x1, waiting for transfers between devices, local(): grad_a, grad_b_cols = lax.psum((local_a, shard_up_weight), 'dp')  250 us
    reduce_scatter x1, waiting for transfers between devices, local(): lax.psum_scatter(head_terms(context, output_weight).astype(jnp.bfloat16),...  92.7 us
    psum x1, blocking collectives, local(): lax.psum(ADAPTER_SCALE * jnp.dot(output_gradient, up_weight_columns.T, pr...  33.9 us
    psum x1, blocking collectives, local(): lax.psum(jnp.dot(context, adapter_down_weight, preferred_element_type=jnp...  32.7 us
    all_gather x1, blocking collectives, local(): grad_b = lax.all_gather(grad_b_cols, 'tensor', axis=1, tiled=True)  29.9 us
  transfers between devices with their start and end apart: 2, of which 2 were waited for; matrix products, arithmetic and copies ran while one was open for 0% of the time, Pallas kernels for 0%

profile of v1, /device:TPU:2, one launch (start us, length us, event | category | flops | bytes accessed | tf_op | source)
XLA Modules:
  0.0 880.8 jit_solution(729789084789001168)
XLA Ops:
  7.2 0.0 copy-start
  7.2 0.0 reduce-scatter.2.cloned.1.call-start
  7.2 1.3 copy.11
  8.5 2.2 stack.2
  10.7 376.0 %all_to_all.5 = bf16[32,1024,256]{1,2,0:T(8,128)(2,1)} all-to-all(bf16[32,1024,256]{1,2,0:T(8,128)(2,1)S(1)} %stack.2), channel_id=1, replica_groups=mesh['dp'=32,'tensor'=8] {'dp'}, dimensions={0} | all-to-all | bytes 33554432 | tf_op jit(solution)/shard_map/all_to_all | solution.py:16
  386.7 0.0 copy-done
  386.7 12.0 %convolution_convert_fusion = bf16[384,8192]{1,0:T(8,128)(2,1)} fusion(bf16[384,1024]{1,0:T(8,128)(2,1)S(1)} %copy-done, bf16[1024,8192]{0,1:T(8,128)(2,1)} %bitcast.17), kind=kOutput, calls=%fused_computation | convolution fusion | flops 6445596672 | bytes 23855104 | tf_op jit(solution)/shard_map/dot_general | solution.py:58
  398.7 0.0 copy-start.3
  398.7 0.0 copy-start.4
  398.7 0.0 copy-start.2
  398.7 0.0 copy-start.1
  398.7 0.0 reduce-scatter.2.cloned.1.call-update
  398.7 0.0 all-reduce.4.cloned.1.call-start
  398.8 0.6 copy-done.3
  399.3 0.6 reduce_sum.54
  399.9 0.6 dynamic_slice.10
  400.5 0.0 copy-done.4
  400.5 0.6 dynamic_slice.11
  401.2 0.6 reduce_sum.58
  404.5 0.0 copy-done.2
  404.5 0.3 fusion.8
  404.8 32.7 %psum.56 = f32[384,16]{0,1:T(8,128)S(1)} all-reduce(f32[384,16]{0,1:T(8,128)S(1)} %fusion.8), channel_id=1, replica_groups=mesh['dp'=32,'tensor'=8] {'tensor'}, use_global_device_ids=true, to_apply=%region_1.0 | all-reduce | flops 6144 | bytes 49152 | tf_op jit(solution)/shard_map/psum | solution.py:79
  437.5 92.7 %reduce-scatter.2.cloned.1.call-done = bf16[384,1024]{1,0:T(8,128)(2,1)} async-done(((bf16[384,8192]{1,0:T(8,128)(2,1)}), bf16[384,1024]{1,0:T(8,128)(2,1)}) %reduce-scatter.2.cloned.1.call-update) | async-done | bytes 786448 | tf_op jit(solution)/shard_map/reduce_scatter | solution.py:82
  530.1 0.0 copy-done.1
  530.1 3.1 multiply_reduce_fusion.1
  533.3 17.2 %all-reduce.1 = (f32[384]{0:T(512)S(1)}, f32[384]{0:T(512)S(1)}, f32[384]{0:T(512)S(1)}, f32[384]{0:T(512)S(1)}) all-reduce(f32[384]{0:T(512)S(1)} %get-tuple-element.4, f32[384]{0:T(512)S(1)} %get-tuple-element.3, f32[384]{0:T(512)S(1)} %get-tuple-element.6, f32[384]{0:T(512)S(1)} %get-tuple-element.5), channel_id=1, replica_groups=mesh['dp'=32,'tensor'=8] {'tensor'}, use_global_device_ids=true, to_apply=%region_11.0 | all-reduce | flops 1536 | bytes 12288 | tf_op jit(solution)/shard_map/psum | solution.py:99
  550.5 0.7 select_divide_fusion
  551.2 2.7 multiply_add_fusion
  553.9 1.6 convolution_multiply_fusion
  555.5 1.5 convolution_multiply_fusion.1
  557.0 33.9 %psum.61 = f32[384,16]{1,0:T(8,128)S(1)} all-reduce(f32[384,16]{1,0:T(8,128)S(1)} %convolution_multiply_fusion), channel_id=1, replica_groups=mesh['dp'=32,'tensor'=8] {'tensor'}, use_global_device_ids=true, to_apply=%region_12.0 | all-reduce | flops 6144 | bytes 49152 | tf_op jit(solution)/shard_map/psum | solution.py:122
  590.9 1.1 convolution_bitcast_fusion
  592.0 0.0 all-reduce.4.cloned.1.call-update
  592.0 249.8 %all-reduce.4.cloned.1.call-done = (f32[1024,16]{0,1:T(8,128)}, f32[16,1024]{1,0:T(8,128)}) async-done(((f32[1024,16]{0,1:T(8,128)}, f32[16,1024]{1,0:T(8,128)}), (f32[1024,16]{0,1:T(8,128)}, f32[16,1024]{1,0:T(8,128)})) %all-reduce.4.cloned.1.call-update) | async-done | bytes 131088 | tf_op jit(solution)/shard_map/psum | solution.py:136
  841.8 29.9 %all_gather.3 = f32[16,8192]{1,0:T(8,128)S(1)} all-gather(f32[16,1024]{1,0:T(8,128)} %get-tuple-element.8), channel_id=1, replica_groups=mesh['dp'=32,'tensor'=8] {'tensor'}, dimensions={1}, use_global_device_ids=true | all-gather | bytes 589824 | tf_op jit(solution)/shard_map/all_gather | solution.py:137
  871.7 1.5 copy.15
  873.2 0.8 copy.16
Async XLA Ops:
  7.2 379.5 %copy-start = (bf16[384,1024]{1,0:T(8,128)(2,1)S(1)}, bf16[384,1024]{1,0:T(8,128)(2,1)}, u32[]{:S(2)}) copy-start(bf16[384,1024]{1,0:T(8,128)(2,1)} %param.8) | copy-start | bytes 2359300
  7.2 522.9 %reduce-scatter.2.cloned.1.call-start = ((), (), s32[]{:S(2)}) async-start(), calls=%async_computation.2 | async-start | bytes 7077888 | tf_op jit(solution)/shard_map/reduce_scatter | solution.py:82
  398.7 0.7 copy-start.3
  398.7 1.9 copy-start.4
  398.7 5.8 copy-start.2
  398.7 131.5 %copy-start.1 = (bf16[384,1024]{1,0:T(8,128)(2,1)S(1)}, bf16[384,1024]{1,0:T(8,128)(2,1)}, u32[]{:S(2)}) copy-start(bf16[384,1024]{1,0:T(8,128)(2,1)} %param.13) | copy-start | bytes 2359300
  398.7 443.1 %all-reduce.4.cloned.1.call-start = ((), (), s32[]{:S(2)}) async-start(), calls=%async_computation.3 | async-start | bytes 262144 | tf_op jit(solution)/shard_map/psum | solution.py:136
Sparse Core Ops, SparseCore 0:
  398.8 131.2 reduce-scatter.1
  592.1 249.6 all-reduce.3
